TPU v7x, 32 devices: a whole 2x2x4 slice. The times are simulated.
32 devices in a mesh: row: 4 (over x, core), col: 8 (over z, y).
Axes of the slice: x: 2, y: 2, z: 4, core: 2. Of those that a mesh axis runs over, the one named last changes fastest.
Arguments:
- signatures: bfloat16 [2048, 49152], P('row', 'col'), as said below
- trailing: float32 [2048, 1024], P('row', 'col'), may hold values from -6 to 6
- ridge: float32 [1], replicated, may hold values from 0.5 to 2
- panel_index: int32 [1], replicated, may hold values from 1 to 3
Outputs:
- factor: float32 [2048, 256], P(('row', 'col'))
- updated: float32 [2048, 1024], P('row', 'col')
Inputs may be any that keep to these rules, and one draw needn't show every extreme that they name: `signatures`: every diagonal block of the Gram matrix plus the ridge is positive definite.
All inputs are finite; a program needn't handle non-finite values.
Results may differ from a plain program's by a relative error of at most 0.0003.
Values may be sent and summed in bfloat16 or wider, within the bound.
A program may use at most 64 MiB of HBM per device.

v0:
```python
import jax
import jax.numpy as jnp
from jax import lax
from jax.sharding import PartitionSpec as P

PANEL = 256


def spread(block, axis, owner):
    block = jnp.where(lax.axis_index(axis) == owner, block, jnp.zeros_like(block))
    return lax.psum(block, axis)


def add_ridge(block, first_row, panel_start, ridge):
    row_ids = first_row + lax.broadcasted_iota(jnp.int32, block.shape, 0)
    col_ids = panel_start + lax.broadcasted_iota(jnp.int32, block.shape, 1)
    return block + jnp.where(row_ids == col_ids, ridge[0], jnp.zeros((), block.dtype))


def mask_above(block, first_row, panel_start):
    row_ids = first_row + lax.broadcasted_iota(jnp.int32, block.shape, 0)
    return jnp.where(row_ids >= panel_start, block, jnp.zeros((), block.dtype))


def solve_rows(lower, panel_rows):
    return jax.scipy.linalg.solve_triangular(lower, panel_rows.T, lower=True).T


def local(signatures, trailing, ridge, panel_index):
    rows_dev = signatures.shape[0]
    tile_cols = trailing.shape[1]
    col_count = lax.axis_size("col")
    row_share = rows_dev // col_count
    row_pos = lax.axis_index("row")
    col_pos = lax.axis_index("col")
    panel_start = panel_index[0] * PANEL
    row_owner = panel_start // rows_dev
    local_offset = panel_start % rows_dev
    own_paths = lax.dynamic_slice_in_dim(signatures, local_offset, PANEL, 0)
    panel_paths = spread(own_paths, "row", row_owner)
    mine_rows = lax.psum_scatter(
        lax.dot_general(
            signatures, panel_paths, (((1,), (1,)), ((), ())), preferred_element_type=jnp.float32
        ),
        "col",
        scatter_dimension=0,
        tiled=True,
    )
    mine_rows = add_ridge(mine_rows, row_pos * rows_dev + col_pos * row_share, panel_start, ridge)
    own_block = lax.dot_general(
        panel_paths, panel_paths, (((1,), (1,)), ((), ())), preferred_element_type=jnp.float32
    )
    diagonal = lax.psum(own_block, "col")
    diagonal = add_ridge(diagonal, panel_start, panel_start, ridge)
    lower = jnp.linalg.cholesky(diagonal)
    factor_mine = solve_rows(lower, mine_rows)
    factor_mine = mask_above(factor_mine, row_pos * rows_dev + col_pos * row_share, panel_start)
    factor_block = lax.all_gather(factor_mine, "col", axis=0, tiled=True)
    window_start = panel_start + PANEL + col_pos * tile_cols
    window_owner = window_start // rows_dev
    window_cut = lax.dynamic_slice_in_dim(factor_block, window_start % rows_dev, tile_cols, 0)
    window_rows = spread(window_cut, "row", window_owner)
    updated = trailing - lax.dot_general(
        factor_block,
        window_rows,
        (((1,), (1,)), ((), ())),
        precision=lax.Precision.HIGHEST,
        preferred_element_type=jnp.float32,
    )
    return (factor_mine, updated)


def solution(mesh):
    placed = (P("row", "col"), P("row", "col"), P(), P())
    return jax.shard_map(
        local,
        mesh=mesh,
        in_specs=placed,
        out_specs=(P(("row", "col"), None), P("row", "col")),
        check_vma=False,
    )
```

profile of v0, /device:TPU:0, one launch (start us, length us, event | category | flops | bytes accessed | tf_op | source)
XLA Modules:
  0.0 299.6 jit_solution(7277814875881397498)
XLA Ops:
  7.9 4.5 %dynamic-slice_select_fusion = bf16[256,6144]{1,0:T(8,128)(2,1)} fusion(bf16[512,6144]{1,0:T(8,128)(2,1)} %param.4, s32[]{:T(128)S(6)} %select_n.62, pred[]{:T(512)S(6)} %eq.15), kind=kLoop, calls=%fused_computation.2 | loop fusion | flops 1572864 | bytes 6291461 | tf_op jit(solution)/shard_map/jit(_where)/select_n | solution.py:10
  13.3 70.5 %all-reduce.5.cloned.1.call-done = bf16[256,6144]{1,0:T(8,128)(2,1)} async-done(((bf16[256,6144]{1,0:T(8,128)(2,1)}), bf16[256,6144]{1,0:T(8,128)(2,1)}) %all-reduce.5.cloned.1.call-update) | async-done | bytes 3145744 | tf_op jit(solution)/shard_map/psum | solution.py:11
  83.8 4.6 %fusion.10 = f32[256,256]{0,1:T(8,128)} fusion(bf16[256,6144]{1,0:T(8,128)(2,1)} %all-reduce.5.cloned.1.call-done), kind=kOutput, calls=%fused_computation.39 | convolution fusion | flops 805306368 | bytes 3407872 | tf_op jit(solution)/shard_map/dot_general | solution.py:50
  88.4 5.6 %convolution_bitcast_fusion = f32[512,256]{0,1:T(8,128)S(1)} fusion(bf16[256,6144]{1,0:T(8,128)(2,1)} %all-reduce.5.cloned.1.call-done, bf16[512,6144]{1,0:T(8,128)(2,1)} %param.4), kind=kOutput, calls=%fused_computation.3 | convolution fusion | flops 1610612736 | bytes 9961472 | tf_op jit(solution)/shard_map/dot_general | solution.py:42
  94.0 1.0 copy.19
  95.2 64.4 %all-reduce.7.cloned.1.call-done = f32[256,256]{0,1:T(8,128)} async-done(((f32[256,256]{0,1:T(8,128)}), f32[256,256]{0,1:T(8,128)}) %all-reduce.7.cloned.1.call-update) | async-done | bytes 262160 | tf_op jit(solution)/shard_map/psum | solution.py:53
  159.6 1.0 select_add_fusion
  160.8 1.1 fusion
  161.9 11.7 %cholesky.49 = f32[128,128]{1,0:T(8,128)S(1)} custom-call(f32[128,128]{1,0:T(8,128)S(1)} %cholesky.115), custom_call_target="Cholesky" | custom-call | tf_op jit(solution)/shard_map/jit(cholesky)/cholesky | solution.py:55
  173.7 9.8 %custom-call.15 = f32[1,128,128]{1,2,0:T(8,128)S(1)} custom-call(f32[1,128,128]{2,1,0:T(8,128)S(1)} %get-tuple-element.29), custom_call_target="InvertDiagBlocksLowerTriangular" | custom-call | tf_op jit(solution)/shard_map/jit(cholesky)/cholesky | solution.py:55
  184.0 11.7 %cholesky.103 = f32[128,128]{1,0:T(8,128)S(1)} custom-call(f32[128,128]{1,0:T(8,128)S(1)} %convolution_subtract_fusion.2), custom_call_target="Cholesky" | custom-call | tf_op jit(solution)/shard_map/jit(cholesky)/cholesky | solution.py:55
  196.0 0.6 compare_reduce_fusion
  198.1 4.4 %while.1 = (s32[]{:T(128)}, f32[256,256]{0,1:T(8,128)S(1)}, s32[2,2]{1,0:T(2,128)S(1)}, f32[2,128,128]{2,1,0:T(8,128)S(1)}, s32[]{:T(128)}) while((s32[]{:T(128)}, f32[256,256]{0,1:T(8,128)S(1)}, s32[2,2]{1,0:T(2,128)S(1)}, f32[2,128,128]{2,1,0:T(8,128)S(1)}, s32[]{:T(128)}) %tuple.27), condition=%wide.while_cond, body=%wide.while_body.sunk | while | flops 2 | bytes 393321 | solution.py:26
  198.3 0.6 fusion.22
  198.9 1.4 dynamic-slice.7
  200.4 0.6 fusion.22
  201.0 1.4 dynamic-slice.7
  202.5 19.7 %custom-call.16 = f32[2,128,128]{1,2,0:T(8,128)S(1)} custom-call(f32[2,128,128]{2,1,0:T(8,128)S(1)} %get-tuple-element.9), custom_call_target="InvertDiagBlocksLowerTriangular" | custom-call | tf_op jit(solution)/shard_map/jit(_solve_triangular)/triangular_solve | solution.py:26
  222.2 3.6 %reduce-scatter.4.cloned.1.call-done = f32[64,256]{1,0:T(8,128)} async-done(((f32[512,256]{1,0:T(8,128)}), f32[64,256]{1,0:T(8,128)}) %reduce-scatter.4.cloned.1.call-update) | async-done | bytes 65552
  225.8 0.9 copy.20
  227.8 31.4 %all_gather.3 = f32[512,256]{1,0:T(8,128)S(1)} all-gather(f32[64,256]{1,0:T(8,128)S(1)} %fusion.7), channel_id=1, replica_groups=mesh['row'=4,'col'=8] {'col'}, dimensions={0}, use_global_device_ids=true | all-gather | bytes 589824 | tf_op jit(solution)/shard_map/all_gather | solution.py:58
  259.2 0.7 dynamic-slice_select_fusion.1
  259.9 30.9 %all-reduce.9.cloned.1.call-done = f32[128,256]{1,0:T(8,128)} async-done(((f32[128,256]{1,0:T(8,128)}), f32[128,256]{1,0:T(8,128)}) %all-reduce.9.cloned.1.call-update) | async-done | bytes 131088 | tf_op jit(solution)/shard_map/psum | solution.py:11
  290.9 2.2 convolution_subtract_fusion
  (42 shorter events, 2.8 us)
Async XLA Ops:
  7.2 76.6 %all-reduce.5.cloned.1.call-start = ((), (), s32[]{:S(2)}) async-start(), calls=%async_computation.1 | async-start | bytes 6291456 | tf_op jit(solution)/shard_map/psum | solution.py:11
  12.5 147.2 %all-reduce.7.cloned.1.call-start = ((), (), s32[]{:S(2)}) async-start(), calls=%async_computation.2 | async-start | bytes 524288 | tf_op jit(solution)/shard_map/psum | solution.py:53
  88.3 137.4 %reduce-scatter.4.cloned.1.call-start = ((), (), s32[]{:S(2)}) async-start(), calls=%async_computation.4 | async-start | bytes 589824
  95.0 195.9 %all-reduce.9.cloned.1.call-start = ((), (), s32[]{:S(2)}) async-start(), calls=%async_computation.3 | async-start | bytes 262144 | tf_op jit(solution)/shard_map/psum | solution.py:11
  183.5 107.4 %copy-start.1 = (f32[512,128]{1,0:T(8,128)S(1)}, f32[512,128]{1,0:T(8,128)}, u32[]{:S(2)}) copy-start(f32[512,128]{1,0:T(8,128)} %param.5) | copy-start | bytes 786436
  227.8 65.3 %copy-start = (f32[64,256]{1,0:T(8,128)}, f32[64,256]{1,0:T(8,128)S(1)}, u32[]{:S(2)}) copy-start(f32[64,256]{1,0:T(8,128)S(1)} %fusion.7) | copy-start | bytes 196612
Sparse Core Ops, SparseCore 0:
  12.6 71.1 all-reduce.4
  88.5 71.1 all-reduce.6
  163.0 62.7 reduce-scatter.3
  260.0 30.7 all-reduce.8
where the time goes:
time: 300 us
  waiting for transfers between devices  169 us (56%)
  other arithmetic  61.2 us (20%)
  blocking collectives  31.4 us (10%)
  between operations  16.7 us (6%)
  matrix products  13.6 us (5%)
  local copies, waits for them, and re-layouts  6.6 us (2%)
    psum x2, waiting for transfers between devices, spread(): return lax.psum(block, axis)  101 us
    psum x1, waiting for transfers between devices, local(): diagonal = lax.psum(own_block, 'col')  64.4 us
    another operation x6, other arithmetic, local(): lower = jnp.linalg.cholesky(diagonal)  34 us
    all_gather x1, blocking collectives, local(): factor_block = lax.all_gather(factor_mine, 'col', axis=0, tiled=True)  31.4 us
    another operation x3, other arithmetic, solve_rows(): return jax.scipy.linalg.solve_triangular(lower, panel_rows.T, lower=True).T  19.7 us
  transfers between devices with their start and end apart: 4, of which 4 were waited for; matrix products, arithmetic and copies ran while one was open for 23% of the time, Pallas kernels for 0%

commit v1 on v0

--- a/solution.py
+++ b/solution.py
@@ -50,7 +50,7 @@
     own_block = lax.dot_general(
         panel_paths, panel_paths, (((1,), (1,)), ((), ())), preferred_element_type=jnp.float32
     )
-    diagonal = lax.psum(own_block, "col")
+    diagonal = jnp.sum(lax.all_gather(own_block, "col"), axis=0)
     diagonal = add_ridge(diagonal, panel_start, panel_start, ridge)
     lower = jnp.linalg.cholesky(diagonal)
     factor_mine = solve_rows(lower, mine_rows)

time: 300 us -> 338 us (1.13)
  waiting for transfers between devices: 169 us -> 209 us
    psum x1 -> x0, waiting for transfers between devices: 64.4 us -> none  [local(): diagonal = lax.psum(own_block, 'col')]
    unnamed x5, waiting for transfers between devices: 3.63 us -> 57.3 us
    all_gather x0 -> x1, waiting for transfers between devices: none -> 49.7 us  [local(): diagonal = jnp.sum(lax.all_gather(own_block, 'col'), axis=0)]
  transfers between devices with their start and end apart: 4 -> 4, of which waited for: 4 -> 4; matrix products, arithmetic and copies ran while one was open for 23% -> 2% of each run, Pallas kernels for 0% -> 0%
where the time goes in v1:
time: 338 us
  waiting for transfers between devices  209 us (62%)
  other arithmetic  61 us (18%)
  blocking collectives  31.4 us (9%)
  between operations  16.6 us (5%)
  matrix products  13.5 us (4%)
  local copies, waits for them, and re-layouts  6.11 us (2%)
    psum x2, waiting for transfers between devices, spread(): return lax.psum(block, axis)  102 us
    unnamed x5, waiting for transfers between devices  57.3 us
    all_gather x1, waiting for transfers between devices, local(): diagonal = jnp.sum(lax.all_gather(own_block, 'col'), axis=0)  49.7 us
    another operation x6, other arithmetic, local(): lower = jnp.linalg.cholesky(diagonal)  33.9 us
    all_gather x1, blocking collectives, local(): factor_block = lax.all_gather(factor_mine, 'col', axis=0, tiled=True)  31.4 us
    another operation x3, other arithmetic, solve_rows(): return jax.scipy.linalg.solve_triangular(lower, panel_rows.T, lower=True).T  19.7 us
  transfers between devices with their start and end apart: 4, of which 4 were waited for; matrix products, arithmetic and copies ran while one was open for 2% of the time, Pallas kernels for 0%

profile of v1, /device:TPU:0, one launch (start us, length us, event | category | flops | bytes accessed | tf_op | source)
XLA Modules:
  0.0 337.9 jit_solution(7236050195148766943)
XLA Ops:
  7.9 4.5 %dynamic-slice_select_fusion = bf16[256,6144]{1,0:T(8,128)(2,1)} fusion(bf16[512,6144]{1,0:T(8,128)(2,1)} %param.4, s32[]{:T(128)S(6)} %select_n.65, pred[]{:T(512)S(6)} %eq.18), kind=kLoop, calls=%fused_computation.2 | loop fusion | flops 1572864 | bytes 6291461 | tf_op jit(solution)/shard_map/jit(_where)/select_n | solution.py:10
  12.5 71.3 %all-reduce.4.cloned.1.call-done = bf16[256,6144]{1,0:T(8,128)(2,1)} async-done(((bf16[256,6144]{1,0:T(8,128)(2,1)}), bf16[256,6144]{1,0:T(8,128)(2,1)}) %all-reduce.4.cloned.1.call-update) | async-done | bytes 3145744 | tf_op jit(solution)/shard_map/psum | solution.py:11
  83.8 5.6 %convolution_bitcast_fusion = f32[512,256]{0,1:T(8,128)S(1)} fusion(bf16[256,6144]{1,0:T(8,128)(2,1)} %all-reduce.4.cloned.1.call-done, bf16[512,6144]{1,0:T(8,128)(2,1)} %param.4), kind=kOutput, calls=%fused_computation.3 | convolution fusion | flops 1610612736 | bytes 9961472 | tf_op jit(solution)/shard_map/dot_general | solution.py:42
  89.3 1.0 copy.8
  90.4 4.6 %fusion.9 = f32[256,256]{1,0:T(8,128)} fusion(bf16[256,6144]{1,0:T(8,128)(2,1)} %all-reduce.4.cloned.1.call-done), kind=kOutput, calls=%fused_computation.37 | convolution fusion | flops 805306368 | bytes 3407872 | tf_op jit(solution)/shard_map/dot_general | solution.py:50
  96.0 57.3 %reduce-scatter.4.cloned.1.call-done = f32[64,256]{1,0:T(8,128)} async-done(((f32[512,256]{1,0:T(8,128)}), f32[64,256]{1,0:T(8,128)}) %reduce-scatter.4.cloned.1.call-update) | async-done | bytes 65552
  153.3 0.9 copy.9
  154.3 49.7 %all-gather.3.cloned.1.call-done = f32[2048,256]{1,0:T(8,128)} async-done(((f32[256,256]{1,0:T(8,128)}), f32[2048,256]{1,0:T(8,128)}) %all-gather.3.cloned.1.call-update) | async-done | bytes 2097168 | tf_op jit(solution)/shard_map/all_gather | solution.py:53
  204.0 1.8 reduce_sum.11
  206.1 11.7 %cholesky.49 = f32[128,128]{1,0:T(8,128)S(1)} custom-call(f32[128,128]{1,0:T(8,128)S(1)} %cholesky.115), custom_call_target="Cholesky" | custom-call | tf_op jit(solution)/shard_map/jit(cholesky)/cholesky | solution.py:55
  217.9 9.8 %custom-call.15 = f32[1,128,128]{1,2,0:T(8,128)S(1)} custom-call(f32[1,128,128]{2,1,0:T(8,128)S(1)} %get-tuple-element.23), custom_call_target="InvertDiagBlocksLowerTriangular" | custom-call | tf_op jit(solution)/shard_map/jit(cholesky)/cholesky | solution.py:55
  228.2 11.7 %cholesky.103 = f32[128,128]{1,0:T(8,128)S(1)} custom-call(f32[128,128]{1,0:T(8,128)S(1)} %convolution_subtract_fusion.2), custom_call_target="Cholesky" | custom-call | tf_op jit(solution)/shard_map/jit(cholesky)/cholesky | solution.py:55
  239.9 0.6 compare_reduce_fusion
  242.0 4.2 %while.1 = (s32[]{:T(128)}, f32[256,256]{1,0:T(8,128)S(1)}, s32[2,2]{1,0:T(2,128)S(1)}, f32[2,128,128]{2,1,0:T(8,128)S(1)}, s32[]{:T(128)}) while((s32[]{:T(128)}, f32[256,256]{1,0:T(8,128)S(1)}, s32[2,2]{1,0:T(2,128)S(1)}, f32[2,128,128]{2,1,0:T(8,128)S(1)}, s32[]{:T(128)}) %tuple.27), condition=%wide.while_cond, body=%wide.while_body.sunk | while | flops 2 | bytes 131181 | solution.py:26
  242.2 0.6 fusion.21
  242.8 1.4 bitcast_dynamic-update-slice_fusion.2
  244.2 0.6 fusion.21
  244.8 1.4 bitcast_dynamic-update-slice_fusion.2
  246.2 19.7 %custom-call.16 = f32[2,128,128]{1,2,0:T(8,128)S(1)} custom-call(f32[2,128,128]{2,1,0:T(8,128)S(1)} %get-tuple-element.9), custom_call_target="InvertDiagBlocksLowerTriangular" | custom-call | tf_op jit(solution)/shard_map/jit(_solve_triangular)/triangular_solve | solution.py:26
  265.8 0.3 fusion.2
  266.7 31.4 %all_gather.11 = f32[512,256]{1,0:T(8,128)S(1)} all-gather(f32[64,256]{1,0:T(8,128)S(1)} %fusion.6), channel_id=1, replica_groups=mesh['row'=4,'col'=8] {'col'}, dimensions={0}, use_global_device_ids=true | all-gather | bytes 589824 | tf_op jit(solution)/shard_map/all_gather | solution.py:58
  298.1 0.7 dynamic-slice_select_fusion.1
  298.8 30.4 %all-reduce.6.cloned.1.call-done = f32[128,256]{1,0:T(8,128)} async-done(((f32[128,256]{1,0:T(8,128)}), f32[128,256]{1,0:T(8,128)}) %all-reduce.6.cloned.1.call-update) | async-done | bytes 131088 | tf_op jit(solution)/shard_map/psum | solution.py:11
  329.2 2.2 convolution_subtract_fusion
  (33 shorter events, 2.1 us)
Async XLA Ops:
  7.2 76.6 %all-reduce.4.cloned.1.call-start = ((), (), s32[]{:S(2)}) async-start(), calls=%async_computation.1 | async-start | bytes 6291456 | tf_op jit(solution)/shard_map/psum | solution.py:11
  12.5 140.8 %reduce-scatter.4.cloned.1.call-start = ((), (), s32[]{:S(2)}) async-start(), calls=%async_computation.4 | async-start | bytes 589824
  90.4 113.7 %all-gather.3.cloned.1.call-start = ((), (), s32[]{:S(2)}) async-start(), calls=%async_computation.3 | async-start | bytes 2359296 | tf_op jit(solution)/shard_map/all_gather | solution.py:53
  95.0 234.2 %all-reduce.6.cloned.1.call-start = ((), (), s32[]{:S(2)}) async-start(), calls=%async_computation.2 | async-start | bytes 262144 | tf_op jit(solution)/shard_map/psum | solution.py:11
  205.8 123.4 %copy-start.1 = (f32[512,128]{1,0:T(8,128)S(1)}, f32[512,128]{1,0:T(8,128)}, u32[]{:S(2)}) copy-start(f32[512,128]{1,0:T(8,128)} %param.5) | copy-start | bytes 786436
  266.7 64.7 %copy-start = (f32[64,256]{1,0:T(8,128)}, f32[64,256]{1,0:T(8,128)S(1)}, u32[]{:S(2)}) copy-start(f32[64,256]{1,0:T(8,128)S(1)} %fusion.6) | copy-start | bytes 196612
Sparse Core Ops, SparseCore 0:
  12.6 71.1 all-reduce.3
  90.5 62.7 reduce-scatter.3
  156.0 48.0 all-gather.2
  298.9 30.2 all-reduce.5
